TPU v7x, 32 devices: a whole 2x2x4 slice. The times are simulated.
32 devices in a mesh: seq: 8 (over z, x), head: 4 (over y, core).
Axes of the slice: x: 2, y: 2, z: 4, core: 2. Of those that a mesh axis runs over, the one named last changes fastest.
Arguments:
- queries: float32 [8192, 4096], P('seq', 'head'), may hold values from -6 to 6
- keys: float32 [8192, 4096], P('seq', 'head'), may hold values from -6 to 6
- values: float32 [8192, 4096], P('seq', 'head'), may hold values from -6 to 6
- out_grad: float32 [8192, 4096], P('seq', 'head'), may hold values from -6 to 6
- inputs: float32 [8192, 4096], P('seq', 'head'), may hold values from -20 to 20
- row_state: float32 [4, 4096], P('head', 'seq'), may hold values from 0.2 to 5
- col_state: float32 [8, 4096], P('seq', 'head'), may hold values from 0.2 to 5
Outputs:
- query_grad: float32 [8192, 4096], P('seq', 'head')
- key_grad: float32 [8192, 4096], P('seq', 'head')
- update: float32 [4096, 4096], P('seq', 'head')
- row_next: float32 [4, 4096], P('head', 'seq')
- col_next: float32 [8, 4096], P('seq', 'head')
All inputs are finite; a program needn't handle non-finite values.
Results may differ from a plain program's by a relative error of at most 0.0001.
Values sent between devices are 32-bit elements; how exact they have to be, the bound alone decides.
No kernel may reach another device: no remote copies, remote signals or barrier semaphores. Data moves between devices by JAX's collectives and lax.ppermute only.
A program may use at most 128 MiB of HBM per device.

v0:
```python
import jax
import jax.numpy as jnp
from jax import lax
from jax.sharding import PartitionSpec as P

HEAD_DIM = 128
highest = lax.Precision.HIGHEST
moment_eps = 1e-06
decay_rate = 0.9


def shards(queries, keys, values, out_grad, inputs, row_state, col_state):
    tok_count, feat_width = queries.shape
    head_count = feat_width // HEAD_DIM
    seq_count = lax.axis_size("seq")
    blk_size = min(512, tok_count)
    num_blocks = tok_count // blk_size
    attn_scale = 1.0 / jnp.sqrt(jnp.float32(HEAD_DIM * tok_count * seq_count))

    def split_blocks(array):
        return array.reshape(num_blocks, blk_size, head_count, HEAD_DIM)

    query_blocks = split_blocks(queries)
    key_blocks = split_blocks(keys)
    value_blocks = split_blocks(values)
    grad_blocks = split_blocks(out_grad)
    rows_idx = lax.broadcasted_iota(jnp.int32, (blk_size, blk_size), 0)
    cols_idx = lax.broadcasted_iota(jnp.int32, (blk_size, blk_size), 1)
    causal_mask = (cols_idx <= rows_idx).astype(jnp.float32)
    grad_value = (
        jnp.einsum("nthd,nshd->nhts", grad_blocks, value_blocks, precision=highest) * causal_mask
    )
    query_key = (
        jnp.einsum("nthd,nshd->nhts", query_blocks, key_blocks, precision=highest) * causal_mask
    )
    block_fwd = jnp.einsum("nsha,nshb->nhab", value_blocks, key_blocks, precision=highest)
    block_rev = jnp.einsum("ntha,nthb->nhab", query_blocks, grad_blocks, precision=highest)
    local_fwd = jnp.sum(block_fwd, axis=0)
    local_rev = jnp.sum(block_rev, axis=0)
    every_fwd, every_rev = (
        lax.all_gather(local_fwd[None], "seq", axis=0, tiled=True),
        lax.all_gather(local_rev[None], "seq", axis=0, tiled=True),
    )
    seq_index = lax.axis_index("seq")
    positions = lax.iota(jnp.int32, every_fwd.shape[0])
    before = (positions < seq_index).astype(jnp.float32)
    after = (positions > seq_index).astype(jnp.float32)
    enter_fwd = jnp.einsum("j,jhab->hab", before, every_fwd, precision=highest)
    enter_rev = jnp.einsum("j,jhab->hab", after, every_rev, precision=highest)
    prefix_fwd = enter_fwd[None] + jnp.cumsum(block_fwd, axis=0) - block_fwd
    suffix_rev = enter_rev[None] + local_rev[None] - jnp.cumsum(block_rev, axis=0)
    query_grad = jnp.einsum("nhts,nshd->nthd", grad_value, key_blocks, precision=highest)
    query_grad = query_grad + jnp.einsum(
        "ntha,nhab->nthb", grad_blocks, prefix_fwd, precision=highest
    )
    key_grad = jnp.einsum("nhts,nthd->nshd", grad_value, query_blocks, precision=highest)
    key_grad = key_grad + jnp.einsum("nshb,nhab->nsha", value_blocks, suffix_rev, precision=highest)
    value_grad = jnp.einsum("nhts,nthd->nshd", query_key, grad_blocks, precision=highest)
    value_grad = value_grad + jnp.einsum(
        "nsha,nhab->nshb", key_blocks, suffix_rev, precision=highest
    )
    query_grad = (attn_scale * query_grad).reshape(tok_count, feat_width)
    key_grad = (attn_scale * key_grad).reshape(tok_count, feat_width)
    value_grad = (attn_scale * value_grad).reshape(tok_count, feat_width)
    value_whole = lax.all_gather(value_grad, "head", axis=1, tiled=True)
    weight_grad = lax.psum_scatter(
        lax.dot_general(
            value_whole,
            inputs,
            (((0,), (0,)), ((), ())),
            precision=highest,
            preferred_element_type=jnp.float32,
        ),
        "seq",
        scatter_dimension=0,
        tiled=True,
    )
    weight_grad = weight_grad / jnp.sqrt(jnp.float32(tok_count * seq_count))
    squares = weight_grad * weight_grad + moment_eps
    row_next = decay_rate * row_state + (1.0 - decay_rate) * jnp.mean(squares, axis=1)[None, :]
    col_next = decay_rate * col_state + (1.0 - decay_rate) * jnp.mean(squares, axis=0)[None, :]
    second = row_next[0][:, None] * col_next[0][None, :] / jnp.mean(row_next)
    update = weight_grad / jnp.sqrt(second)
    return (query_grad, key_grad, update, row_next, col_next)


def solution(mesh):
    in_specs = (
        P("seq", "head"),
        P("seq", "head"),
        P("seq", "head"),
        P("seq", "head"),
        P("seq", "head"),
        P("head", "seq"),
        P("seq", "head"),
    )
    out_specs = (
        P("seq", "head"),
        P("seq", "head"),
        P("seq", "head"),
        P("head", "seq"),
        P("seq", "head"),
    )
    return jax.shard_map(shards, mesh=mesh, in_specs=in_specs, out_specs=out_specs, check_vma=False)
```

profile of v0, /device:TPU:0, one launch (start us, length us, event | category | flops | bytes accessed | tf_op | source)
XLA Modules:
  0.0 588.8 jit_solution(3645238673202636491)
XLA Ops:
  7.2 3.4 copy.90
  12.7 8.4 %fusion.57 = (f32[8,128,128]{2,1,0:T(8,128)}, f32[2,8,128,128]{3,2,1,0:T(8,128)S(1)}) fusion(f32[2,512,8,128]{3,2,1,0:T(8,128)S(1)} %bitcast.70, f32[2,512,8,128]{3,2,1,0:T(8,128)S(1)} %bitcast.81), kind=kOutput, calls=%fused_computation.66 | convolution fusion | flops 1610743808 | bytes 9961472 | tf_op jit(solution)/shard_map/ntha,nthb->nhab/dot_general | solution.py:37
  21.4 3.4 copy.92
  26.7 16.0 %fusion.18 = f32[2,8,512,512]{3,2,1,0:T(8,128)} fusion(f32[2,512,8,128]{3,2,1,0:T(8,128)S(1)} %bitcast.83, f32[2,512,8,128]{3,2,1,0:T(8,128)S(1)} %bitcast.74), kind=kOutput, calls=%fused_computation.24 | convolution fusion | flops 6442450944 | bytes 25165824 | tf_op jit(solution)/shard_map/nthd,nshd->nhts/dot_general | solution.py:34
  42.6 31.1 %fusion = f32[2,8,512,128]{3,2,1,0:T(8,128)} fusion(f32[2,8,512,512]{3,2,1,0:T(8,128)} %fusion.18, f32[512,512]{1,0:T(8,128)S(1)} %fusion.46, f32[2,512,8,128]{3,2,1,0:T(8,128)S(1)} %bitcast.72), kind=kOutput, calls=%fused_computation | convolution fusion | flops 6446645248 | bytes 26214400 | tf_op jit(solution)/shard_map/nhts,nthd->nshd/dot_general | solution.py:58
  73.7 23.1 %all-gather.10.cloned.1.call-done = f32[64,128,128]{2,1,0:T(8,128)} async-done(((f32[8,128,128]{2,1,0:T(8,128)}), f32[64,128,128]{2,1,0:T(8,128)}) %all-gather.10.cloned.1.call-update) | async-done | bytes 4194320 | tf_op jit(solution)/shard_map/all_gather | solution.py:42
  96.8 6.6 %fusion.12 = f32[1,8,128,128]{3,0,2,1:T(1,128)S(1)} fusion(f32[8,8,128,128]{3,2,1,0:T(8,128)} %bitcast.89, s32[]{:T(128)S(6)} %axis_index.15), kind=kOutput, calls=%fused_computation.18 | convolution fusion | flops 12582920 | bytes 4718596 | tf_op jit(solution)/shard_map/j,jhab->hab/dot_general | solution.py:49
  103.8 4.4 fusion.9
  108.2 2.4 copy.76
  110.6 2.9 copy.146
  114.1 3.4 copy.91
  117.5 9.5 %fusion.56 = (f32[8,128,128]{2,1,0:T(8,128)}, f32[2,8,128,128]{3,2,1,0:T(8,128)}) fusion(f32[2,512,8,128]{3,2,1,0:T(8,128)S(1)} %bitcast.77, f32[2,512,8,128]{3,2,1,0:T(8,128)S(1)} %bitcast.78), kind=kOutput, calls=%fused_computation.65 | convolution fusion | flops 1610743808 | bytes 9961472 | tf_op jit(solution)/shard_map/nsha,nshb->nhab/dot_general | solution.py:36
  127.1 91.1 %all-gather.6.cloned.1.call-done = f32[1024,4096]{1,0:T(8,128)} async-done(((f32[1024,1024]{1,0:T(8,128)}), f32[1024,4096]{1,0:T(8,128)}) %all-gather.6.cloned.1.call-update) | async-done | bytes 16777232 | tf_op jit(solution)/shard_map/all_gather | solution.py:65
  218.2 59.7 %fusion.58 = f32[4096,1024]{1,0:T(8,128)} fusion(f32[1024,4096]{1,0:T(8,128)} %all-gather.6.cloned.1.call-done, f32[1024,1024]{1,0:T(8,128)} %param.11), kind=kOutput, calls=%fused_computation.67 | convolution fusion | flops 51539607552 | bytes 37748736 | tf_op jit(solution)/shard_map/dot_general | solution.py:67
  277.9 18.8 %fusion.25 = f32[2,8,512,512]{3,2,1,0:T(8,128)S(1)} fusion(f32[2,512,8,128]{3,2,1,0:T(8,128)} %bitcast.79, f32[2,512,8,128]{3,2,1,0:T(8,128)} %bitcast.71), kind=kOutput, calls=%fused_computation.31 | convolution fusion | flops 6442450944 | bytes 25165824 | tf_op jit(solution)/shard_map/nthd,nshd->nhts/dot_general | solution.py:31
  296.8 30.1 %fusion.2 = f32[2,8,512,128]{3,2,1,0:T(8,128)} fusion(f32[2,8,512,512]{3,2,1,0:T(8,128)S(1)} %fusion.25, f32[512,512]{1,0:T(8,128)S(1)} %fusion.46, f32[2,512,8,128]{3,2,1,0:T(8,128)} %bitcast.82), kind=kOutput, calls=%fused_computation.2 | convolution fusion | flops 6446645248 | bytes 26214400 | tf_op jit(solution)/shard_map/nhts,nthd->nshd/dot_general | solution.py:56
  326.8 18.3 %fusion.4 = f32[2,8,512,128]{3,2,1,0:T(8,128)} fusion(f32[2,8,512,512]{3,2,1,0:T(8,128)S(1)} %fusion.25, f32[512,512]{1,0:T(8,128)S(1)} %fusion.46, f32[2,512,8,128]{3,2,1,0:T(8,128)} %bitcast.75), kind=kOutput, calls=%fused_computation.4 | convolution fusion | flops 6446645248 | bytes 26214400 | tf_op jit(solution)/shard_map/nhts,nshd->nthd/dot_general | solution.py:52
  345.1 7.7 %fusion.10 = f32[2,512,8,128]{3,1,2,0:T(8,128)S(1)} fusion(f32[2,8,512,128]{3,2,1,0:T(8,128)} %fusion.2, f32[2,8,128,128]{3,2,1,0:T(8,128)} %copy-done.13, f32[2,512,8,128]{3,2,1,0:T(8,128)} %bitcast.80), kind=kOutput, calls=%fused_computation.15 | convolution fusion | flops 1612709888 | bytes 13631488 | tf_op jit(solution)/shard_map/nshb,nhab->nsha/dot_general | solution.py:57
  352.8 4.4 copy.68
  357.3 6.6 %fusion.14 = f32[1,8,128,128]{3,0,2,1:T(1,128)S(1)} fusion(f32[8,8,128,128]{3,2,1,0:T(8,128)} %bitcast.88, s32[]{:T(128)S(6)} %axis_index.15), kind=kOutput, calls=%fused_computation.20 | convolution fusion | flops 12582920 | bytes 4718596 | tf_op jit(solution)/shard_map/j,jhab->hab/dot_general | solution.py:48
  364.5 4.4 fusion.11
  371.4 5.5 copy_bitcast_fusion.1
  376.9 198.2 %reduce-scatter.2.cloned.1.call-done = f32[512,1024]{1,0:T(8,128)} async-done(((f32[4096,1024]{1,0:T(8,128)}), f32[512,1024]{1,0:T(8,128)}) %reduce-scatter.2.cloned.1.call-update) | async-done | bytes 2097168 | tf_op jit(solution)/shard_map/reduce_scatter | solution.py:66
  578.5 3.3 rsqrt_multiply_fusion
  (60 shorter events, 10.9 us)
Async XLA Ops:
  7.2 89.6 %all-gather.10.cloned.1.call-start = ((), (), s32[]{:S(2)}) async-start(), calls=%async_computation.4 | async-start | bytes 4718592 | tf_op jit(solution)/shard_map/all_gather | solution.py:42
  7.2 3.5 copy-start.15
  10.6 2.1 copy-start
  11.7 9.4 %copy-start.7 = (f32[128,8,8,128]{3,2,1,0:T(8,128)}, f32[128,8,8,128]{3,2,1,0:T(8,128)S(1)}, u32[]{:S(2)}) copy-start(f32[128,8,8,128]{3,2,1,0:T(8,128)S(1)} %copy.94) | copy-start | bytes 12582916
  21.1 197.1 %all-gather.6.cloned.1.call-start = ((), (), s32[]{:S(2)}) async-start(), calls=%async_computation.1 | async-start | bytes 20971520 | tf_op jit(solution)/shard_map/all_gather | solution.py:65
  21.3 5.3 copy-start.8
  24.7 2.0 copy-start.3
  26.7 16.0 %copy-start.1 = (f32[128,8,8,128]{3,2,1,0:T(8,128)S(1)}, f32[128,8,8,128]{3,2,1,0:T(8,128)}, u32[]{:S(2)}) copy-start(f32[128,8,8,128]{3,2,1,0:T(8,128)} %copy-done) | copy-start | bytes 12582916
  73.7 29.7 %copy-start.14 = (f32[8,128,128]{2,1,0:T(8,128)S(1)}, f32[8,128,128]{2,1,0:T(8,128)}, u32[]{:S(2)}) copy-start(f32[8,128,128]{2,1,0:T(8,128)} %get-tuple-element.11) | copy-start | bytes 1572868
  96.8 6.9 %copy-start.4 = (f32[128,8,8,128]{3,2,1,0:T(8,128)S(1)}, f32[128,8,8,128]{3,2,1,0:T(8,128)}, u32[]{:S(2)}) copy-start(f32[128,8,8,128]{3,2,1,0:T(8,128)} %copy-done.3) | copy-start | bytes 12582916
  96.8 6.9 %copy-start.11 = (f32[2,8,512,128]{3,2,1,0:T(8,128)S(1)}, f32[2,8,512,128]{3,2,1,0:T(8,128)}, u32[]{:S(2)}) copy-start(f32[2,8,512,128]{3,2,1,0:T(8,128)} %fusion) | copy-start | bytes 12582916
  103.7 4.4 copy-start.13
  113.6 243.7 %all-gather.8.cloned.1.call-start = ((), (), s32[]{:S(2)}) async-start(), calls=%async_computation.3 | async-start | bytes 4718592 | tf_op jit(solution)/shard_map/all_gather | solution.py:41
  114.1 3.5 copy-start.5
  117.4 9.5 %copy-start.6 = (f32[128,8,8,128]{3,2,1,0:T(8,128)}, f32[128,8,8,128]{3,2,1,0:T(8,128)S(1)}, u32[]{:S(2)}) copy-start(f32[128,8,8,128]{3,2,1,0:T(8,128)S(1)} %copy.91) | copy-start | bytes 12582916
  127.0 448.1 %reduce-scatter.2.cloned.1.call-start = ((), (), s32[]{:S(2)}) async-start(), calls=%async_computation.2 | async-start | bytes 18874368 | tf_op jit(solution)/shard_map/reduce_scatter | solution.py:66
  352.8 11.1 %copy-start.12 = (f32[2,8,128,128]{3,2,1,0:T(8,128)S(1)}, f32[2,8,128,128]{3,2,1,0:T(8,128)}, u32[]{:S(2)}) copy-start(f32[2,8,128,128]{3,2,1,0:T(8,128)} %get-tuple-element.10) | copy-start | bytes 3145732
  357.3 7.2 %copy-start.2 = (f32[128,8,8,128]{3,2,1,0:T(8,128)S(1)}, f32[128,8,8,128]{3,2,1,0:T(8,128)}, u32[]{:S(2)}) copy-start(f32[128,8,8,128]{3,2,1,0:T(8,128)} %copy-done) | copy-start | bytes 12582916
  357.3 7.2 %copy-start.9 = (f32[2,8,512,128]{3,2,1,0:T(8,128)S(1)}, f32[2,8,512,128]{3,2,1,0:T(8,128)}, u32[]{:S(2)}) copy-start(f32[2,8,512,128]{3,2,1,0:T(8,128)} %fusion.4) | copy-start | bytes 12582916
  368.9 2.5 copy-start.10
  371.4 205.8 %copy-start.19 = (f32[1,512]{1,0:T(1,128)S(1)}, f32[1,512]{1,0:T(1,128)}, u32[]{:S(2)}) copy-start(f32[1,512]{1,0:T(1,128)} %param.12) | copy-start | bytes 6148
  371.4 207.1 %copy-start.18 = (f32[1,1024]{1,0:T(1,128)S(1)}, f32[1,1024]{1,0:T(1,128)}, u32[]{:S(2)}) copy-start(f32[1,1024]{1,0:T(1,128)} %param.13) | copy-start | bytes 12292
  577.8 4.0 copy-start.17
  578.5 3.3 copy-start.16
Sparse Core Ops, SparseCore 0:
  21.2 75.5 all-gather.9
  113.7 104.4 all-gather.5
  220.3 72.7 all-gather.7
  296.8 278.2 reduce-scatter.1
where the time goes:
time: 596 us; the launch traced here: 589 us
  waiting for transfers between devices  313 us (53%)
  matrix products  222 us (37%)
  local copies, waits for them, and re-layouts  31.8 us (5%)
  between operations  15.2 us (3%)
  other arithmetic  6.94 us (1%)
    reduce_scatter x1, waiting for transfers between devices, shards(): lax.psum_scatter(lax.dot_general(value_whole, inputs, (((0,), (0,)), ((),...  198 us
    all_gather x1, waiting for transfers between devices, shards(): value_whole = lax.all_gather(value_grad, 'head', axis=1, tiled=True)  91.1 us
    dot_general x1, matrix products, shards(): lax.dot_general(value_whole, inputs, (((0,), (0,)), ((), ())), precision=...  59.7 us
    dot_general x1, matrix products, shards(): jnp.einsum('nhts,nthd->nshd', query_key, grad_blocks, precision=highest)  31.1 us
    dot_general x1, matrix products, shards(): jnp.einsum('nhts,nthd->nshd', grad_value, query_blocks, precision=highest)  30.1 us
    all_gather x1, waiting for transfers between devices, shards(): lax.all_gather(local_rev[None], 'seq', axis=0, tiled=True)  23.1 us
    dot_general x1, matrix products, shards(): jnp.einsum('nthd,nshd->nhts', grad_blocks, value_blocks, precision=highest)  18.8 us
    dot_general x1, matrix products, shards(): jnp.einsum('nhts,nshd->nthd', grad_value, key_blocks, precision=highest)  18.3 us
  transfers between devices with their start and end apart: 4, of which 3 were waited for; matrix products, arithmetic and copies ran while one was open for 38% of the time, Pallas kernels for 0%

commit v1 on v0

--- a/solution.py
+++ b/solution.py
@@ -62,7 +62,14 @@
     query_grad = (attn_scale * query_grad).reshape(tok_count, feat_width)
     key_grad = (attn_scale * key_grad).reshape(tok_count, feat_width)
     value_grad = (attn_scale * value_grad).reshape(tok_count, feat_width)
-    value_whole = lax.all_gather(value_grad, "head", axis=1, tiled=True)
+    ways, here = (lax.axis_size("head"), lax.axis_index("head"))
+    value_whole, reach = (value_grad, 1)
+    while reach < ways:
+        theirs = lax.ppermute(value_whole, "head", [(d, d ^ reach) for d in range(ways)])
+        mine_first = jnp.concatenate([value_whole, theirs], axis=1)
+        theirs_first = jnp.concatenate([theirs, value_whole], axis=1)
+        value_whole = jnp.where(here & reach == 0, mine_first, theirs_first)
+        reach = 2 * reach
     weight_grad = lax.psum_scatter(
         lax.dot_general(
             value_whole,

time: 596 us -> 677 us (1.14)
  waiting for transfers between devices: 313 us -> 378 us
  other arithmetic: 6.94 us -> 17.4 us
    ppermute x0 -> x2, waiting for transfers between devices: none -> 177 us  [shards(): lax.ppermute(value_whole, 'head', [(d, d ^ reach) for d in range(ways)])]
    all_gather x1 -> x0, waiting for transfers between devices: 91.1 us -> none  [shards(): value_whole = lax.all_gather(value_grad, 'head', axis=1, tiled=True)]
    reduce_scatter x1, waiting for transfers between devices: 198 us -> 179 us  [shards(): lax.psum_scatter(lax.dot_general(value_whole, inputs, (((0,), (0,)), ((),...]
    select_n x0 -> x1, other arithmetic: none -> 10.5 us  [shards(): value_whole = jnp.where(here & reach == 0, mine_first, theirs_first)]
    unnamed x45 -> x47, local copies, waits for them, and re-layouts: 17.1 us -> 16.4 us
  transfers between devices with their start and end apart: 4 -> 5, of which waited for: 3 -> 4; matrix products, arithmetic and copies ran while one was open for 38% -> 33% of each run, Pallas kernels for 0% -> 0%
where the time goes in v1:
time: 677 us; the launch traced here: 670 us
  waiting for transfers between devices  378 us (56%)
  matrix products  226 us (33%)
  local copies, waits for them, and re-layouts  31.2 us (5%)
  other arithmetic  17.4 us (3%)
  between operations  15 us (2%)
    reduce_scatter x1, waiting for transfers between devices, shards(): lax.psum_scatter(lax.dot_general(value_whole, inputs, (((0,), (0,)), ((),...  179 us
    ppermute x2, waiting for transfers between devices, shards(): lax.ppermute(value_whole, 'head', [(d, d ^ reach) for d in range(ways)])  177 us
    dot_general x1, matrix products, shards(): lax.dot_general(value_whole, inputs, (((0,), (0,)), ((), ())), precision=...  63.2 us
    dot_general x1, matrix products, shards(): jnp.einsum('nhts,nthd->nshd', query_key, grad_blocks, precision=highest)  31 us
    dot_general x1, matrix products, shards(): jnp.einsum('nhts,nthd->nshd', grad_value, query_blocks, precision=highest)  30.5 us
    all_gather x1, waiting for transfers between devices, shards(): lax.all_gather(local_rev[None], 'seq', axis=0, tiled=True)  22.8 us
    dot_general x1, matrix products, shards(): jnp.einsum('nthd,nshd->nhts', grad_blocks, value_blocks, precision=highest)  18.9 us
    dot_general x1, matrix products, shards(): jnp.einsum('nhts,nshd->nthd', grad_value, key_blocks, precision=highest)  18.3 us
  transfers between devices with their start and end apart: 5, of which 4 were waited for; matrix products, arithmetic and copies ran while one was open for 33% of the time, Pallas kernels for 0%

profile of v1, /device:TPU:0, one launch (start us, length us, event | category | flops | bytes accessed | tf_op | source)
XLA Modules:
  0.0 669.7 jit_solution(12100726112617702734)
XLA Ops:
  7.2 3.4 copy.90
  12.7 8.4 %fusion.65 = (f32[8,128,128]{2,1,0:T(8,128)}, f32[2,8,128,128]{3,2,1,0:T(8,128)S(1)}) fusion(f32[2,512,8,128]{3,2,1,0:T(8,128)S(1)} %bitcast.70, f32[2,512,8,128]{3,2,1,0:T(8,128)S(1)} %bitcast.81), kind=kOutput, calls=%fused_computation.76 | convolution fusion | flops 1610743808 | bytes 9961472 | tf_op jit(solution)/shard_map/ntha,nthb->nhab/dot_general | solution.py:37
  21.7 3.4 copy.92
  27.0 16.0 %fusion.25 = f32[2,8,512,512]{3,2,1,0:T(8,128)} fusion(f32[2,512,8,128]{3,2,1,0:T(8,128)S(1)} %bitcast.83, f32[2,512,8,128]{3,2,1,0:T(8,128)S(1)} %bitcast.74), kind=kOutput, calls=%fused_computation.33 | convolution fusion | flops 6442450944 | bytes 25165824 | tf_op jit(solution)/shard_map/nthd,nshd->nhts/dot_general | solution.py:34
  42.9 31.0 %fusion.6 = f32[2,8,512,128]{3,2,1,0:T(8,128)} fusion(f32[2,8,512,512]{3,2,1,0:T(8,128)} %fusion.25, f32[512,512]{1,0:T(8,128)S(1)} %fusion.53, f32[2,512,8,128]{3,2,1,0:T(8,128)S(1)} %bitcast.72), kind=kOutput, calls=%fused_computation.7 | convolution fusion | flops 6446645248 | bytes 26214400 | tf_op jit(solution)/shard_map/nhts,nthd->nshd/dot_general | solution.py:58
  74.0 22.8 %all-gather.7.cloned.1.call-done = f32[64,128,128]{2,1,0:T(8,128)} async-done(((f32[8,128,128]{2,1,0:T(8,128)}), f32[64,128,128]{2,1,0:T(8,128)}) %all-gather.7.cloned.1.call-update) | async-done | bytes 4194320 | tf_op jit(solution)/shard_map/all_gather | solution.py:42
  96.8 6.6 fusion.19
  103.8 4.4 fusion.16
  110.6 3.0 copy.146
  113.6 7.5 %collective-permute-done = f32[1024,1024]{1,0:T(8,128)} collective-permute-done((f32[1024,1024]{1,0:T(8,128)}, f32[1024,1024]{1,0:T(8,128)}, u32[]{:S(2)}, u32[]{:S(2)}) %collective-permute-start) | collective-permute-done | bytes 4194336 | tf_op jit(solution)/shard_map/ppermute | solution.py:68
  121.1 10.5 %maximum_select_fusion.2 = f32[1024,2048]{1,0:T(8,128)} fusion(f32[1024,1024]{1,0:T(8,128)} %collective-permute-done, f32[1024,1024]{1,0:T(8,128)} %bitcast.69, pred[]{:T(512)S(6)} %eq.7), kind=kLoop, calls=%fused_computation.13 | loop fusion | flops 6291456 | bytes 16777216 | tf_op jit(solution)/shard_map/jit(_where)/select_n | solution.py:71
  135.9 9.5 %fusion.64 = (f32[8,128,128]{2,1,0:T(8,128)}, f32[2,8,128,128]{3,2,1,0:T(8,128)}) fusion(f32[2,512,8,128]{3,2,1,0:T(8,128)S(1)} %bitcast.77, f32[2,512,8,128]{3,2,1,0:T(8,128)S(1)} %bitcast.78), kind=kOutput, calls=%fused_computation.75 | convolution fusion | flops 1610743808 | bytes 9961472 | tf_op jit(solution)/shard_map/nsha,nshb->nhab/dot_general | solution.py:36
  145.4 169.1 %collective-permute-done.1 = f32[1024,2048]{1,0:T(8,128)} collective-permute-done((f32[1024,2048]{1,0:T(8,128)}, f32[1024,2048]{1,0:T(8,128)}, u32[]{:S(2)}, u32[]{:S(2)}) %collective-permute-start.1) | collective-permute-done | bytes 8388640 | tf_op jit(solution)/shard_map/ppermute | solution.py:68
  314.5 63.2 %fusion = f32[4096,1024]{1,0:T(8,128)} fusion(f32[1024,1024]{1,0:T(8,128)} %param.11, f32[1024,2048]{1,0:T(8,128)} %collective-permute-done.1, f32[1024,2048]{1,0:T(8,128)} %maximum_select_fusion.2, pred[]{:T(512)S(6)} %eq.6), kind=kOutput, calls=%fused_computation.1 | convolution fusion | flops 51552190464 | bytes 37748736 | tf_op jit(solution)/shard_map/dot_general | solution.py:74
  377.7 18.9 %fusion.32 = f32[2,8,512,512]{3,2,1,0:T(8,128)S(1)} fusion(f32[2,512,8,128]{3,2,1,0:T(8,128)} %bitcast.79, f32[2,512,8,128]{3,2,1,0:T(8,128)} %bitcast.71), kind=kOutput, calls=%fused_computation.40 | convolution fusion | flops 6442450944 | bytes 25165824 | tf_op jit(solution)/shard_map/nthd,nshd->nhts/dot_general | solution.py:31
  396.6 30.5 %fusion.8 = f32[2,8,512,128]{3,2,1,0:T(8,128)} fusion(f32[2,8,512,512]{3,2,1,0:T(8,128)S(1)} %fusion.32, f32[512,512]{1,0:T(8,128)S(1)} %fusion.53, f32[2,512,8,128]{3,2,1,0:T(8,128)} %bitcast.82), kind=kOutput, calls=%fused_computation.9 | convolution fusion | flops 6446645248 | bytes 26214400 | tf_op jit(solution)/shard_map/nhts,nthd->nshd/dot_general | solution.py:56
  427.2 18.3 %fusion.10 = f32[2,8,512,128]{3,2,1,0:T(8,128)} fusion(f32[2,8,512,512]{3,2,1,0:T(8,128)S(1)} %fusion.32, f32[512,512]{1,0:T(8,128)S(1)} %fusion.53, f32[2,512,8,128]{3,2,1,0:T(8,128)} %bitcast.75), kind=kOutput, calls=%fused_computation.11 | convolution fusion | flops 6446645248 | bytes 26214400 | tf_op jit(solution)/shard_map/nhts,nshd->nthd/dot_general | solution.py:52
  445.5 7.8 %fusion.17 = f32[2,512,8,128]{3,1,2,0:T(8,128)S(1)} fusion(f32[2,8,512,128]{3,2,1,0:T(8,128)} %fusion.8, f32[2,8,128,128]{3,2,1,0:T(8,128)} %copy-done.13, f32[2,512,8,128]{3,2,1,0:T(8,128)} %bitcast.80), kind=kOutput, calls=%fused_computation.24 | convolution fusion | flops 1612709888 | bytes 13631488 | tf_op jit(solution)/shard_map/nshb,nhab->nsha/dot_general | solution.py:57
  453.3 4.4 copy.68
  457.7 6.7 fusion.21
  464.9 4.4 fusion.18
  471.8 5.5 copy_bitcast_fusion.1
  477.3 178.9 %reduce-scatter.2.cloned.1.call-done = f32[512,1024]{1,0:T(8,128)} async-done(((f32[4096,1024]{1,0:T(8,128)}), f32[512,1024]{1,0:T(8,128)}) %reduce-scatter.2.cloned.1.call-update) | async-done | bytes 2097168 | tf_op jit(solution)/shard_map/reduce_scatter | solution.py:73
  659.6 3.3 rsqrt_multiply_fusion
  (64 shorter events, 17.2 us)
Async XLA Ops:
  7.2 89.6 %all-gather.7.cloned.1.call-start = ((), (), s32[]{:S(2)}) async-start(), calls=%async_computation.3 | async-start | bytes 4718592 | tf_op jit(solution)/shard_map/all_gather | solution.py:42
  7.2 3.5 copy-start.15
  11.7 9.4 %copy-start.7 = (f32[128,8,8,128]{3,2,1,0:T(8,128)}, f32[128,8,8,128]{3,2,1,0:T(8,128)S(1)}, u32[]{:S(2)}) copy-start(f32[128,8,8,128]{3,2,1,0:T(8,128)S(1)} %copy.94) | copy-start | bytes 12582916
  21.1 436.6 %all-gather.5.cloned.1.call-start = ((), (), s32[]{:S(2)}) async-start(), calls=%async_computation.2 | async-start | bytes 4718592 | tf_op jit(solution)/shard_map/all_gather | solution.py:41
  21.6 5.3 copy-start.8
  27.0 16.0 %copy-start.1 = (f32[128,8,8,128]{3,2,1,0:T(8,128)S(1)}, f32[128,8,8,128]{3,2,1,0:T(8,128)}, u32[]{:S(2)}) copy-start(f32[128,8,8,128]{3,2,1,0:T(8,128)} %copy-done) | copy-start | bytes 12582916
  74.0 29.4 %copy-start.14 = (f32[8,128,128]{2,1,0:T(8,128)S(1)}, f32[8,128,128]{2,1,0:T(8,128)}, u32[]{:S(2)}) copy-start(f32[8,128,128]{2,1,0:T(8,128)} %get-tuple-element.11) | copy-start | bytes 1572868
  96.8 6.9 %copy-start.4 = (f32[128,8,8,128]{3,2,1,0:T(8,128)S(1)}, f32[128,8,8,128]{3,2,1,0:T(8,128)}, u32[]{:S(2)}) copy-start(f32[128,8,8,128]{3,2,1,0:T(8,128)} %copy-done.3) | copy-start | bytes 12582916
  96.8 6.9 %copy-start.11 = (f32[2,8,512,128]{3,2,1,0:T(8,128)S(1)}, f32[2,8,512,128]{3,2,1,0:T(8,128)}, u32[]{:S(2)}) copy-start(f32[2,8,512,128]{3,2,1,0:T(8,128)} %fusion.6) | copy-start | bytes 12582916
  103.7 4.4 copy-start.13
  113.6 7.5 %collective-permute-start = (f32[1024,1024]{1,0:T(8,128)}, f32[1024,1024]{1,0:T(8,128)}, u32[]{:S(2)}, u32[]{:S(2)}) collective-permute-start(f32[1024,1024]{1,0:T(8,128)} %bitcast.69), channel_id=1, source_target_pairs={{0,1},{1,0},{2,3},{3,2},{4,5},{5,4},{6,7},{7,6},{8,9},{9,8},{10,11... | collective-permute-start | bytes 12582920 | tf_op jit(solution)/shard_map/ppermute | solution.py:68
  113.6 19.5 %copy-start.16 = (f32[1024,1024]{1,0:T(8,128)S(1)}, f32[1024,1024]{1,0:T(8,128)}, u32[]{:S(2)}) copy-start(f32[1024,1024]{1,0:T(8,128)} %param.9) | copy-start | bytes 12582916
  131.6 182.9 %collective-permute-start.1 = (f32[1024,2048]{1,0:T(8,128)}, f32[1024,2048]{1,0:T(8,128)}, u32[]{:S(2)}, u32[]{:S(2)}) collective-permute-start(f32[1024,2048]{1,0:T(8,128)} %maximum_select_fusion.2), channel_id=1, source_target_pairs={{0,2},{1,3},{2,0},{3,1},{4,6},{5,7},{6,4},{7,5},{8,10},{9,11},{10,... | collective-permute-start | bytes 25165832 | tf_op jit(solution)/shard_map/ppermute | solution.py:68
  133.2 2.7 copy-start.5
  134.2 11.1 %copy-start.6 = (f32[128,8,8,128]{3,2,1,0:T(8,128)}, f32[128,8,8,128]{3,2,1,0:T(8,128)S(1)}, u32[]{:S(2)}) copy-start(f32[128,8,8,128]{3,2,1,0:T(8,128)S(1)} %copy.91) | copy-start | bytes 12582916
  145.3 510.9 %reduce-scatter.2.cloned.1.call-start = ((), (), s32[]{:S(2)}) async-start(), calls=%async_computation.1 | async-start | bytes 18874368 | tf_op jit(solution)/shard_map/reduce_scatter | solution.py:73
  453.3 11.1 %copy-start.12 = (f32[2,8,128,128]{3,2,1,0:T(8,128)S(1)}, f32[2,8,128,128]{3,2,1,0:T(8,128)}, u32[]{:S(2)}) copy-start(f32[2,8,128,128]{3,2,1,0:T(8,128)} %get-tuple-element.10) | copy-start | bytes 3145732
  457.7 7.2 %copy-start.2 = (f32[128,8,8,128]{3,2,1,0:T(8,128)S(1)}, f32[128,8,8,128]{3,2,1,0:T(8,128)}, u32[]{:S(2)}) copy-start(f32[128,8,8,128]{3,2,1,0:T(8,128)} %copy-done) | copy-start | bytes 12582916
  457.7 7.2 %copy-start.9 = (f32[2,8,512,128]{3,2,1,0:T(8,128)S(1)}, f32[2,8,512,128]{3,2,1,0:T(8,128)}, u32[]{:S(2)}) copy-start(f32[2,8,512,128]{3,2,1,0:T(8,128)} %fusion.10) | copy-start | bytes 12582916
  469.4 2.5 copy-start.10
  471.8 186.5 %copy-start.20 = (f32[1,512]{1,0:T(1,128)S(1)}, f32[1,512]{1,0:T(1,128)}, u32[]{:S(2)}) copy-start(f32[1,512]{1,0:T(1,128)} %param.12) | copy-start | bytes 6148
  471.8 187.7 %copy-start.19 = (f32[1,1024]{1,0:T(1,128)S(1)}, f32[1,1024]{1,0:T(1,128)}, u32[]{:S(2)}) copy-start(f32[1,1024]{1,0:T(1,128)} %param.13) | copy-start | bytes 12292
  658.9 4.0 copy-start.18
  659.6 3.3 copy-start.17
  (2 other events, 4.0 us)
Sparse Core Ops, SparseCore 0:
  21.2 75.4 all-gather.6
  145.5 70.4 all-gather.4
  377.9 278.2 reduce-scatter.1
